TPU v7x, 128 devices: a whole 4x4x4 slice. The times are simulated.
128 devices in a mesh: frames: 2 (over y_hi), codebook: 16 (over y_lo, x, core), hidden: 4 (over z).
Axes of the slice: x: 4, y: 4 (y_hi: 2, y_lo: 2; y = y_hi * 2 + y_lo), z: 4, core: 2. Of those that a mesh axis runs over, the one named last changes fastest.
Arguments:
- temporal: bfloat16 [4096, 4096], P(('frames', 'codebook'), 'hidden'), may hold values from -6 to 6
- frame_ids: int32 [4096, 16], P('frames', 'codebook'), may hold values from 0 to 2047
- proj_weight: bfloat16 [16, 4096, 1024], P('codebook', 'hidden'), may hold values from -0.09375 to 0.09375
- embed_table: bfloat16 [16, 2049, 1024], P('codebook'), may hold values from -6 to 6
- qkv_weight: bfloat16 [16, 3, 1024, 1024], P('codebook', None, None, 'hidden'), may hold values from -12 to 12
- out_weight: bfloat16 [16, 1024, 1024], P('codebook', 'hidden'), may hold values from -0.1875 to 0.1875
- gate_up: bfloat16 [16, 2, 1024, 4096], P('codebook', None, None, 'hidden'), may hold values from -0.1875 to 0.1875
- down_weight: bfloat16 [16, 4096, 1024], P('codebook', 'hidden'), may hold values from -0.09375 to 0.09375
- norm_gains: float32 [16, 2, 1024], P('codebook'), may hold values from 0.25 to 1.75
Outputs:
- depth_states: float32 [16, 4096, 1024], P('codebook', 'frames', 'hidden')
All inputs are finite; a program needn't handle non-finite values.
Results may differ from a plain program's by a relative error of at most 0.015.
Values may be sent and summed in bfloat16 or wider, within the bound.
A program may use at most 192 MiB of HBM per device.

v0:
```python
import jax
import jax.numpy as jnp
from jax import lax
from jax.sharding import PartitionSpec as P

HEADS = 16


def shifted(block, axis, distance):
    devices = range(lax.axis_size(axis))
    route = [(i - distance, i) for i in devices if i - distance in devices]
    return lax.ppermute(block, axis, route)


def normalize(values, norm_gain):
    return values * lax.rsqrt(jnp.mean(values * values, axis=-1, keepdims=True) + 1e-05) * norm_gain


def gated(normed, piece):
    gate_sum = jnp.dot(normed, piece[0], preferred_element_type=jnp.float32)
    upper_sum = jnp.dot(normed, piece[1], preferred_element_type=jnp.float32)
    return (jax.nn.silu(gate_sum) * upper_sum).astype(jnp.bfloat16)


def body(
    temporal,
    frame_ids,
    proj_weight,
    embed_table,
    qkv_weight,
    out_weight,
    gate_up,
    down_weight,
    norm_gains,
):
    code_index = lax.axis_index("codebook")
    hidden_index = lax.axis_index("hidden")
    hidden_count = lax.axis_size("hidden")
    start_id = embed_table.shape[1] - 1
    token_table = embed_table[0]
    norm_gain = norm_gains[0]
    earlier = shifted(frame_ids, "codebook", 1)[:, 0]
    previous = jnp.where(code_index == 0, start_id, earlier)
    partial_sum = jnp.dot(
        lax.all_gather(temporal, "codebook", axis=0, tiled=True),
        proj_weight[0],
        preferred_element_type=jnp.float32,
    )
    row_count = partial_sum.shape[0]
    x_zero = lax.psum(partial_sum.astype(jnp.bfloat16), "hidden").astype(jnp.float32) + token_table[
        previous
    ].astype(jnp.float32)
    normed = normalize(x_zero, norm_gain[0]).astype(jnp.bfloat16)
    local_width = qkv_weight.shape[3]
    local_heads = HEADS // hidden_count
    head_size = local_width // local_heads
    triple = jnp.einsum(
        "rd,kdc->krc", normed, qkv_weight[0], preferred_element_type=jnp.float32
    ).astype(jnp.bfloat16)
    query_heads = triple[0].reshape(row_count, local_heads, head_size)
    highest = jnp.full((row_count, local_heads), -1e30, jnp.float32)
    key_piece = lax.all_gather(triple[1][None], "codebook", axis=0, tiled=True)
    value_piece = lax.all_gather(triple[2][None], "codebook", axis=0, tiled=True)
    positions = key_piece.shape[0]
    key_heads = key_piece.reshape(positions, row_count, local_heads, head_size)
    value_heads = value_piece.reshape(positions, row_count, local_heads, head_size)
    scores = jnp.einsum(
        "fhd,jfhd->jfh", query_heads, key_heads, preferred_element_type=jnp.float32
    ) * head_size ** (-0.5)
    valid = (jnp.arange(positions, dtype=jnp.int32) <= code_index)[:, None, None]
    scores = jnp.where(valid, scores, -1e30)
    new_highest = jnp.maximum(highest, jnp.max(scores, axis=0))
    weights = jnp.where(valid, jnp.exp(scores - new_highest[None]), 0.0)
    running = jnp.sum(weights, axis=0)
    summed = jnp.einsum(
        "jfh,jfhd->fhd",
        weights.astype(jnp.bfloat16),
        value_heads,
        preferred_element_type=jnp.float32,
    )
    highest, running, summed = (new_highest, running, summed)
    attended = (summed / running[..., None]).reshape(row_count, local_width).astype(jnp.bfloat16)
    attention_part = jnp.dot(attended, out_weight[0], preferred_element_type=jnp.float32)
    residual = x_zero + lax.psum(attention_part.astype(jnp.bfloat16), "hidden").astype(jnp.float32)
    normed_two = normalize(residual, norm_gain[1]).astype(jnp.bfloat16)
    activated = gated(normed_two, gate_up[0])
    down_part = jnp.dot(activated, down_weight[0], preferred_element_type=jnp.float32)
    mlp_piece = lax.psum_scatter(
        down_part.astype(jnp.bfloat16), "hidden", scatter_dimension=1, tiled=True
    ).astype(jnp.float32)
    own_residual = lax.dynamic_slice_in_dim(residual, hidden_index * local_width, local_width, 1)
    return (own_residual + mlp_piece)[None]


def solution(mesh):
    placed = (
        P(("frames", "codebook"), "hidden"),
        P("frames", "codebook"),
        P("codebook", "hidden", None),
        P("codebook", None, None),
        P("codebook", None, None, "hidden"),
        P("codebook", "hidden", None),
        P("codebook", None, None, "hidden"),
        P("codebook", "hidden", None),
        P("codebook", None, None),
    )
    return jax.shard_map(
        body,
        mesh=mesh,
        in_specs=placed,
        out_specs=P("codebook", "frames", "hidden"),
        check_vma=False,
    )
```

profile of v0, /device:TPU:1, one launch (start us, length us, event | category | flops | bytes accessed | tf_op | source)
XLA Modules:
  0.0 563.1 jit_solution(17674491881883395552)
XLA Ops:
  6.5 0.0 copy-start
  6.5 0.0 all-gather.4.cloned.1.call-start
  6.5 0.7 all-gather.4.cloned.1.call-update
  7.3 0.0 all-reduce.3.cloned.1.call-start
  7.3 42.5 %all-gather.4.cloned.1.call-done = bf16[2048,1024]{1,0:T(8,128)(2,1)} async-done(((bf16[128,1024]{1,0:T(8,128)(2,1)}), bf16[2048,1024]{1,0:T(8,128)(2,1)}) %all-gather.4.cloned.1.call-update) | async-done | bytes 4194320 | tf_op jit(solution)/shard_map/all_gather | solution.py:45
  49.8 0.0 copy-done
  49.8 8.3 %convolution_convert_fusion.2 = bf16[2048,1024]{1,0:T(8,128)(2,1)} fusion(bf16[2048,1024]{1,0:T(8,128)(2,1)} %all-gather.4.cloned.1.call-done, bf16[1,1024,1024]{2,1,0:T(8,128)(2,1)S(1)} %copy-done), kind=kOutput, calls=%fused_computation.16 | convolution fusion | flops 4297064448 | bytes 10485760 | tf_op jit(solution)/shard_map/dot_general | solution.py:44
  58.2 0.0 copy-start.9
  58.2 0.0 copy-start.6
  58.2 0.0 all-reduce.3.cloned.1.call-update
  58.2 0.0 all-gather.6.cloned.1.call-start
  58.2 0.6 copy-done.9
  58.9 2.8 collective-permute-start
  61.7 0.0 copy-done.6
  61.8 0.7 collective-permute-done
  62.5 0.0 copy-start.8
  62.5 13.8 %gather_fusion = bf16[2048,1024]{1,0:T(8,128)(2,1)} fusion(bf16[2049,1024]{1,0:T(8,128)(2,1)} %bitcast.66, s32[2048]{0:T(1024)S(1)} %broadcast_clamp_fusion), kind=kCustom, calls=%fused_computation | custom fusion | bytes 8396800 | tf_op jit(solution)/shard_map/gather | solution.py:50
  76.3 74.6 %all-reduce.3.cloned.1.call-done = bf16[2048,1024]{1,0:T(8,128)(2,1)} async-done(((bf16[2048,1024]{1,0:T(8,128)(2,1)}), bf16[2048,1024]{1,0:T(8,128)(2,1)}) %all-reduce.3.cloned.1.call-update) | async-done | bytes 4194320 | tf_op jit(solution)/shard_map/psum | solution.py:50
  150.9 0.0 copy-start.2
  150.9 0.0 copy-start.3
  150.9 5.0 multiply_reduce_fusion.3
  155.9 0.0 copy-done.8
  156.0 0.0 copy-done.2
  156.0 0.9 copy-done.3
  156.8 4.2 fusion.8
  161.0 0.3 fusion.30
  161.3 1.3 copy.21
  162.7 0.0 all-gather.6.cloned.1.call-update
  162.7 0.0 all-gather.8.cloned.1.call-start
  162.7 1.3 copy.23
  164.1 0.0 all-gather.8.cloned.1.call-update
  164.1 0.2 all-reduce.5.cloned.1.call-start
  164.3 0.2 convert.1
  164.6 90.1 %all-gather.6.cloned.1.call-done = bf16[16,2048,256]{2,1,0:T(8,128)(2,1)} async-done(((bf16[1,2048,256]{2,1,0:T(8,128)(2,1)}), bf16[16,2048,256]{2,1,0:T(8,128)(2,1)}) %all-gather.6.cloned.1.call-update) | async-done | bytes 16777232 | tf_op jit(solution)/shard_map/all_gather | solution.py:62
  254.7 22.0 %copy.40 = bf16[16,2048,256]{1,2,0:T(8,128)(2,1)} copy(bf16[16,2048,256]{2,1,0:T(8,128)(2,1)} %all-gather.6.cloned.1.call-done) | data formatting | bytes 33554432
  276.7 7.9 %multiply_reduce_fusion.1 = f32[2048,4,16]{0,1,2:T(4,128)S(1)} fusion(f32[2048,4,64]{0,2,1:T(8,128)S(1)} %convert.1, bf16[16,2048,256]{1,2,0:T(8,128)(2,1)} %copy.40), kind=kLoop, calls=%fused_computation.2 | loop fusion | flops 25034752 | bytes 19398656
  284.5 0.4 bitcast_reduce_fusion
  284.9 0.5 fusion.25
  285.4 0.3 copy.43
  285.8 62.8 %all-gather.8.cloned.1.call-done = bf16[16,2048,256]{2,1,0:T(8,128)(2,1)} async-done(((bf16[1,2048,256]{2,1,0:T(8,128)(2,1)}), bf16[16,2048,256]{2,1,0:T(8,128)(2,1)}) %all-gather.8.cloned.1.call-update) | async-done | bytes 16777232 | tf_op jit(solution)/shard_map/all_gather | solution.py:63
  348.6 21.7 %copy.41 = bf16[16,2048,256]{1,2,0:T(8,128)(2,1)} copy(bf16[16,2048,256]{2,1,0:T(8,128)(2,1)} %all-gather.8.cloned.1.call-done) | data formatting | bytes 33554432
  370.3 0.0 copy-start.5
  370.3 7.7 %multiply_reduce_fusion = f32[2048,4,64]{0,2,1:T(8,128)S(1)} fusion(bf16[2048,4,16,64]{0,3,1,2:T(8,128)(2,1)} %bitcast.67, f32[2048,4,16]{0,1,2:T(4,128)S(1)} %copy.43), kind=kLoop, calls=%fused_computation.1 | loop fusion | flops 24641536 | bytes 19398656 | tf_op jit(solution)/shard_map/jfh,jfhd->fhd/dot_general | solution.py:75
  377.9 0.2 divide_convert_fusion
  378.1 0.0 copy-done.5
  378.1 3.3 convolution_convert_fusion
  381.4 0.0 all-reduce.5.cloned.1.call-update
  381.4 0.0 reduce-scatter.2.cloned.1.call-start
  381.5 93.4 %all-reduce.5.cloned.1.call-done = bf16[2048,1024]{1,0:T(8,128)(2,1)} async-done(((bf16[2048,1024]{1,0:T(8,128)(2,1)}), bf16[2048,1024]{1,0:T(8,128)(2,1)}) %all-reduce.5.cloned.1.call-update) | async-done | bytes 4194320 | tf_op jit(solution)/shard_map/psum | solution.py:84
  474.9 0.0 copy-start.7
  474.9 5.8 %multiply_reduce_fusion.2 = (f32[2048]{0:T(1024)S(1)}, f32[2048,1024]{1,0:T(8,128)S(1)}) fusion(bf16[2048,1024]{1,0:T(8,128)(2,1)} %all-reduce.5.cloned.1.call-done, bf16[2048,1024]{1,0:T(8,128)(2,1)} %gather_fusion, bf16[2048,1024]{1,0:T(8,128)(2,1)} %all-reduce.3.cloned.1.call-done), kind=kLoop, calls=%fused_computation.5 | loop fusion | flops 14678016 | bytes 20979712 | tf_op jit(solution)/shard_map/reduce_sum | solution.py:16
  480.7 0.0 copy-start.4
  480.7 3.2 copy-done.4
  483.9 0.0 copy-done.7
  483.9 6.7 %fusion.14 = f32[2048,1024]{1,0:T(8,128)} fusion(bf16[1,2,1024,1024]{3,2,1,0:T(8,128)(2,1)S(1)} %copy-done.7, f32[2048,1024]{1,0:T(8,128)S(1)} %get-tuple-element.6, f32[1024]{0:T(1024)S(1)} %bitcast.71, f32[2048]{0:T(1024)S(1)} %add_rsqrt_fusion), kind=kOutput, calls=%fused_computation.21 | convolution fusion | flops 4301258752 | bytes 18886656 | tf_op jit(solution)/shard_map/dot_general | solution.py:20
  490.6 15.1 %convolution_convert_fusion.1 = bf16[2048,1024]{1,0:T(8,128)(2,1)} fusion(f32[2048,1024]{1,0:T(8,128)} %fusion.14, bf16[1,1024,1024]{2,1,0:T(8,128)(2,1)} %param.16, bf16[1,2,1024,1024]{3,2,1,0:T(8,128)(2,1)} %param.15, f32[2048,1024]{1,0:T(8,128)} %copy-done.4, f32[1024]{0:T(1024)S(1)} %bitcast.72, f32[2048]{0:T(1024)S(1)} %add_rsqrt_fusion), kind=kOutput, calls=%fused_computation.15 | convolution fusion | flops 8610906112 | bytes 25178112 | tf_op jit(solution)/shard_map/dot_general | solution.py:87
  505.8 0.0 copy-start.1
  505.8 0.0 reduce-scatter.2.cloned.1.call-update
  505.8 47.0 %reduce-scatter.2.cloned.1.call-done = bf16[2048,256]{1,0:T(8,128)(2,1)} async-done(((bf16[2048,1024]{1,0:T(8,128)(2,1)}), bf16[2048,256]{1,0:T(8,128)(2,1)}) %reduce-scatter.2.cloned.1.call-update) | async-done | bytes 1048592 | tf_op jit(solution)/shard_map/reduce_scatter | solution.py:88
  552.9 3.4 add_bitcast_fusion
  556.3 0.0 copy-done.1
  (7 shorter events, 0.1 us)
Async XLA Ops:
  6.5 43.3 %copy-start = (bf16[1,1024,1024]{2,1,0:T(8,128)(2,1)S(1)}, bf16[1,1024,1024]{2,1,0:T(8,128)(2,1)}, u32[]{:S(2)}) copy-start(bf16[1,1024,1024]{2,1,0:T(8,128)(2,1)} %param.11) | copy-start | bytes 6291460
  6.5 43.3 %all-gather.4.cloned.1.call-start = ((), (), s32[]{:S(2)}) async-start(), calls=%async_computation.1 | async-start | bytes 4456448 | tf_op jit(solution)/shard_map/all_gather | solution.py:45
  7.3 143.6 %all-reduce.3.cloned.1.call-start = ((), (), s32[]{:S(2)}) async-start(), calls=%async_computation.2 | async-start | bytes 8388608 | tf_op jit(solution)/shard_map/psum | solution.py:50
  58.2 0.7 copy-start.9
  58.2 3.5 copy-start.6
  58.2 196.5 %all-gather.6.cloned.1.call-start = ((), (), s32[]{:S(2)}) async-start(), calls=%async_computation.3 | async-start | bytes 17825792 | tf_op jit(solution)/shard_map/all_gather | solution.py:62
  58.9 3.6 collective-permute-start
  62.5 93.4 %copy-start.8 = (bf16[1,3,1024,256]{3,2,1,0:T(8,128)(2,1)S(1)}, bf16[1,3,1024,256]{3,2,1,0:T(8,128)(2,1)}, u32[]{:S(2)}) copy-start(bf16[1,3,1024,256]{3,2,1,0:T(8,128)(2,1)} %param.13) | copy-start | bytes 4718596
  150.9 5.1 copy-start.2
  150.9 5.9 %copy-start.3 = (bf16[2048,1024]{1,0:T(8,128)(2,1)S(1)}, bf16[2048,1024]{1,0:T(8,128)(2,1)}, u32[]{:S(2)}) copy-start(bf16[2048,1024]{1,0:T(8,128)(2,1)} %all-reduce.3.cloned.1.call-done) | copy-start | bytes 12582916
  162.7 185.9 %all-gather.8.cloned.1.call-start = ((), (), s32[]{:S(2)}) async-start(), calls=%async_computation.4 | async-start | bytes 17825792 | tf_op jit(solution)/shard_map/all_gather | solution.py:63
  164.1 310.8 %all-reduce.5.cloned.1.call-start = ((), (), s32[]{:S(2)}) async-start(), calls=%async_computation.5 | async-start | bytes 8388608 | tf_op jit(solution)/shard_map/psum | solution.py:84
  370.3 7.9 %copy-start.5 = (bf16[1,256,1024]{2,1,0:T(8,128)(2,1)S(1)}, bf16[1,256,1024]{2,1,0:T(8,128)(2,1)}, u32[]{:S(2)}) copy-start(bf16[1,256,1024]{2,1,0:T(8,128)(2,1)} %param.14) | copy-start | bytes 1572868
  381.4 171.4 %reduce-scatter.2.cloned.1.call-start = ((), (), s32[]{:S(2)}) async-start(), calls=%async_computation.6 | async-start | bytes 5242880 | tf_op jit(solution)/shard_map/reduce_scatter | solution.py:88
  474.9 9.1 %copy-start.7 = (bf16[1,2,1024,1024]{3,2,1,0:T(8,128)(2,1)S(1)}, bf16[1,2,1024,1024]{3,2,1,0:T(8,128)(2,1)}, u32[]{:S(2)}) copy-start(bf16[1,2,1024,1024]{3,2,1,0:T(8,128)(2,1)} %param.15) | copy-start | bytes 12582916
  480.7 3.2 copy-start.4
  505.8 50.5 %copy-start.1 = (bf16[1,1024,1024]{2,1,0:T(8,128)(2,1)S(1)}, bf16[1,1024,1024]{2,1,0:T(8,128)(2,1)}, u32[]{:S(2)}) copy-start(bf16[1,1024,1024]{2,1,0:T(8,128)(2,1)} %param.11) | copy-start | bytes 6291460
Sparse Core Ops, SparseCore 0:
  9.0 40.7 all-gather.3
  58.3 92.5 all-reduce.2
  162.8 91.8 all-gather.5
  256.2 92.3 all-gather.7
  381.6 93.2 all-reduce.4
  505.9 46.8 reduce-scatter.1
where the time goes:
time: 564 us; the launch traced here: 563 us
  waiting for transfers between devices  412 us (73%)
  local copies, waits for them, and re-layouts  65.5 us (12%)
  matrix products  37.6 us (7%)
  other arithmetic  31.1 us (6%)
  between operations  13.7 us (2%)
    psum x1, waiting for transfers between devices, body(): lax.psum(attention_part.astype(jnp.bfloat16), 'hidden').astype(jnp.float32)  93.4 us
    all_gather x1, waiting for transfers between devices, body(): key_piece = lax.all_gather(triple[1][None], 'codebook', axis=0, tiled=True)  90.1 us
    psum x1, waiting for transfers between devices, body(): lax.psum(partial_sum.astype(jnp.bfloat16), 'hidden').astype(jnp.float32)  74.6 us
    all_gather x1, waiting for transfers between devices, body(): lax.all_gather(triple[2][None], 'codebook', axis=0, tiled=True)  62.8 us
    unnamed x23, local copies, waits for them, and re-layouts  48.7 us
    reduce_scatter x1, waiting for transfers between devices, body(): lax.psum_scatter(down_part.astype(jnp.bfloat16), 'hidden', scatter_dimens...  47 us
    all_gather x1, waiting for transfers between devices, body(): lax.all_gather(temporal, 'codebook', axis=0, tiled=True)  42.5 us
    dot_general x1, matrix products, body(): jnp.dot(activated, down_weight[0], preferred_element_type=jnp.float32)  15.1 us
  transfers between devices with their start and end apart: 7, of which 7 were waited for; matrix products, arithmetic and copies ran while one was open for 8% of the time, Pallas kernels for 0%

commit v1 on v0

--- a/solution.py
+++ b/solution.py
@@ -1,9 +1,18 @@
+import functools
 import jax
 import jax.numpy as jnp
 from jax import lax
 from jax.sharding import PartitionSpec as P
 
 HEADS = 16
+
+
+def _match_tracks(row_data, bus_axis):
+    raw_out = lax.all_gather(row_data, bus_axis)
+    return jnp.sum(raw_out, axis=0)
+
+
+cover_kinds = functools.partial(_match_tracks, bus_axis="hidden")
 
 
 def shifted(block, axis, distance):
@@ -81,7 +90,7 @@
     highest, running, summed = (new_highest, running, summed)
     attended = (summed / running[..., None]).reshape(row_count, local_width).astype(jnp.bfloat16)
     attention_part = jnp.dot(attended, out_weight[0], preferred_element_type=jnp.float32)
-    residual = x_zero + lax.psum(attention_part.astype(jnp.bfloat16), "hidden").astype(jnp.float32)
+    residual = x_zero + cover_kinds(attention_part.astype(jnp.bfloat16)).astype(jnp.float32)
     normed_two = normalize(residual, norm_gain[1]).astype(jnp.bfloat16)
     activated = gated(normed_two, gate_up[0])
     down_part = jnp.dot(activated, down_weight[0], preferred_element_type=jnp.float32)

time: 564 us -> 639 us (1.13)
  waiting for transfers between devices: 412 us -> 474 us
  other arithmetic: 31.1 us -> 43.2 us
    all_gather x0 -> x1, waiting for transfers between devices: none -> 154 us  [_match_tracks(): raw_out = lax.all_gather(row_data, bus_axis)]
    psum x1 -> x0, waiting for transfers between devices: 93.4 us -> none  [body(): lax.psum(attention_part.astype(jnp.bfloat16), 'hidden').astype(jnp.float32)]
    reduce_sum x0 -> x1, other arithmetic: none -> 12.1 us  [_match_tracks(): return jnp.sum(raw_out, axis=0)]
  transfers between devices with their start and end apart: 7 -> 7, of which waited for: 7 -> 7; matrix products, arithmetic and copies ran while one was open for 8% -> 7% of each run, Pallas kernels for 0% -> 0%
where the time goes in v1:
time: 639 us; the launch traced here: 637 us
  waiting for transfers between devices  474 us (74%)
  local copies, waits for them, and re-layouts  65.5 us (10%)
  other arithmetic  43.2 us (7%)
  matrix products  37.6 us (6%)
  between operations  13.7 us (2%)
    all_gather x1, waiting for transfers between devices, _match_tracks(): raw_out = lax.all_gather(row_data, bus_axis)  154 us
    all_gather x1, waiting for transfers between devices, body(): key_piece = lax.all_gather(triple[1][None], 'codebook', axis=0, tiled=True)  90.1 us
    psum x1, waiting for transfers between devices, body(): lax.psum(partial_sum.astype(jnp.bfloat16), 'hidden').astype(jnp.float32)  74.6 us
    all_gather x1, waiting for transfers between devices, body(): lax.all_gather(triple[2][None], 'codebook', axis=0, tiled=True)  62.8 us
    unnamed x23, local copies, waits for them, and re-layouts  48.7 us
    reduce_scatter x1, waiting for transfers between devices, body(): lax.psum_scatter(down_part.astype(jnp.bfloat16), 'hidden', scatter_dimens...  48.2 us
    all_gather x1, waiting for transfers between devices, body(): lax.all_gather(temporal, 'codebook', axis=0, tiled=True)  42.5 us
    dot_general x1, matrix products, body(): jnp.dot(activated, down_weight[0], preferred_element_type=jnp.float32)  15.1 us
  transfers between devices with their start and end apart: 7, of which 7 were waited for; matrix products, arithmetic and copies ran while one was open for 7% of the time, Pallas kernels for 0%

profile of v1, /device:TPU:1, one launch (start us, length us, event | category | flops | bytes accessed | tf_op | source)
XLA Modules:
  0.0 637.4 jit_solution(15942974898449882378)
XLA Ops:
  6.5 0.0 copy-start
  6.5 0.0 all-gather.6.cloned.1.call-start
  6.5 0.7 all-gather.6.cloned.1.call-update
  7.3 0.0 all-reduce.2.cloned.1.call-start
  7.3 42.5 %all-gather.6.cloned.1.call-done = bf16[2048,1024]{1,0:T(8,128)(2,1)} async-done(((bf16[128,1024]{1,0:T(8,128)(2,1)}), bf16[2048,1024]{1,0:T(8,128)(2,1)}) %all-gather.6.cloned.1.call-update) | async-done | bytes 4194320 | tf_op jit(solution)/shard_map/all_gather | solution.py:54
  49.8 0.0 copy-done
  49.8 8.3 %convolution_convert_fusion.2 = bf16[2048,1024]{1,0:T(8,128)(2,1)} fusion(bf16[2048,1024]{1,0:T(8,128)(2,1)} %all-gather.6.cloned.1.call-done, bf16[1,1024,1024]{2,1,0:T(8,128)(2,1)S(1)} %copy-done), kind=kOutput, calls=%fused_computation.16 | convolution fusion | flops 4297064448 | bytes 10485760 | tf_op jit(solution)/shard_map/dot_general | solution.py:53
  58.2 0.0 copy-start.9
  58.2 0.0 copy-start.6
  58.2 0.0 all-reduce.2.cloned.1.call-update
  58.2 0.0 all-gather.8.cloned.1.call-start
  58.2 0.6 copy-done.9
  58.9 2.8 collective-permute-start
  61.7 0.0 copy-done.6
  61.8 0.7 collective-permute-done
  62.5 0.0 copy-start.8
  62.5 13.8 %gather_fusion = bf16[2048,1024]{1,0:T(8,128)(2,1)} fusion(bf16[2049,1024]{1,0:T(8,128)(2,1)} %bitcast.67, s32[2048]{0:T(1024)S(1)} %broadcast_clamp_fusion), kind=kCustom, calls=%fused_computation | custom fusion | bytes 8396800 | tf_op jit(solution)/shard_map/gather | solution.py:59
  76.3 74.6 %all-reduce.2.cloned.1.call-done = bf16[2048,1024]{1,0:T(8,128)(2,1)} async-done(((bf16[2048,1024]{1,0:T(8,128)(2,1)}), bf16[2048,1024]{1,0:T(8,128)(2,1)}) %all-reduce.2.cloned.1.call-update) | async-done | bytes 4194320 | tf_op jit(solution)/shard_map/psum | solution.py:59
  150.9 0.0 copy-start.2
  150.9 0.0 copy-start.3
  150.9 5.0 multiply_reduce_fusion.3
  155.9 0.0 copy-done.8
  156.0 0.0 copy-done.2
  156.0 0.9 copy-done.3
  156.8 4.2 fusion.8
  161.0 0.3 fusion.30
  161.3 1.3 copy.21
  162.7 0.0 all-gather.8.cloned.1.call-update
  162.7 0.0 all-gather.10.cloned.1.call-start
  162.7 1.3 copy.23
  164.1 0.0 all-gather.10.cloned.1.call-update
  164.1 0.2 all-gather.12.cloned.1.call-start
  164.3 0.2 convert.2
  164.6 90.1 %all-gather.8.cloned.1.call-done = bf16[16,2048,256]{2,1,0:T(8,128)(2,1)} async-done(((bf16[1,2048,256]{2,1,0:T(8,128)(2,1)}), bf16[16,2048,256]{2,1,0:T(8,128)(2,1)}) %all-gather.8.cloned.1.call-update) | async-done | bytes 16777232 | tf_op jit(solution)/shard_map/all_gather | solution.py:71
  254.7 22.0 %copy.40 = bf16[16,2048,256]{1,2,0:T(8,128)(2,1)} copy(bf16[16,2048,256]{2,1,0:T(8,128)(2,1)} %all-gather.8.cloned.1.call-done) | data formatting | bytes 33554432
  276.7 7.9 %multiply_reduce_fusion.1 = f32[2048,4,16]{0,1,2:T(4,128)S(1)} fusion(f32[2048,4,64]{0,2,1:T(8,128)S(1)} %convert.2, bf16[16,2048,256]{1,2,0:T(8,128)(2,1)} %copy.40), kind=kLoop, calls=%fused_computation.2 | loop fusion | flops 25034752 | bytes 19398656
  284.5 0.4 bitcast_reduce_fusion
  284.9 0.5 fusion.25
  285.4 0.3 copy.43
  285.8 62.8 %all-gather.10.cloned.1.call-done = bf16[16,2048,256]{2,1,0:T(8,128)(2,1)} async-done(((bf16[1,2048,256]{2,1,0:T(8,128)(2,1)}), bf16[16,2048,256]{2,1,0:T(8,128)(2,1)}) %all-gather.10.cloned.1.call-update) | async-done | bytes 16777232 | tf_op jit(solution)/shard_map/all_gather | solution.py:72
  348.6 21.7 %copy.41 = bf16[16,2048,256]{1,2,0:T(8,128)(2,1)} copy(bf16[16,2048,256]{2,1,0:T(8,128)(2,1)} %all-gather.10.cloned.1.call-done) | data formatting | bytes 33554432
  370.3 0.0 copy-start.5
  370.3 7.7 %multiply_reduce_fusion = f32[2048,4,64]{0,2,1:T(8,128)S(1)} fusion(bf16[2048,4,16,64]{0,3,1,2:T(8,128)(2,1)} %bitcast.68, f32[2048,4,16]{0,1,2:T(4,128)S(1)} %copy.43), kind=kLoop, calls=%fused_computation.1 | loop fusion | flops 24641536 | bytes 19398656 | tf_op jit(solution)/shard_map/jfh,jfhd->fhd/dot_general | solution.py:84
  377.9 0.2 divide_convert_fusion
  378.1 0.0 copy-done.5
  378.1 3.2 convolution_convert_fusion
  381.4 0.0 all-gather.12.cloned.1.call-update
  381.4 0.3 reduce-scatter.2.cloned.1.call-start
  381.7 154.2 %all-gather.12.cloned.1.call-done = bf16[8192,1024]{1,0:T(8,128)(2,1)} async-done(((bf16[2048,1024]{1,0:T(8,128)(2,1)}), bf16[8192,1024]{1,0:T(8,128)(2,1)}) %all-gather.12.cloned.1.call-update) | async-done | bytes 16777232 | tf_op jit(solution)/shard_map/all_gather | solution.py:11
  535.9 12.1 %reduce_sum.41 = bf16[2048,1024]{1,0:T(8,128)(2,1)} reduce(bf16[4,2048,1024]{2,1,0:T(8,128)(2,1)} %bitcast.69, bf16[]{:T(256)} %constant.35.clone.1), dimensions={0}, to_apply=%region_4.5 | reduce | flops 6291456 | bytes 20971522 | tf_op jit(solution)/shard_map/reduce_sum | solution.py:12
  547.9 0.0 copy-start.7
  547.9 5.8 multiply_reduce_fusion.2
  553.8 0.0 copy-start.4
  553.8 3.2 copy-done.4
  557.0 0.0 copy-done.7
  557.0 6.8 %fusion.14 = f32[2048,1024]{1,0:T(8,128)} fusion(bf16[1,2,1024,1024]{3,2,1,0:T(8,128)(2,1)S(1)} %copy-done.7, f32[2048,1024]{1,0:T(8,128)S(1)} %get-tuple-element.6, f32[1024]{0:T(1024)S(1)} %bitcast.73, f32[2048]{0:T(1024)S(1)} %add_rsqrt_fusion), kind=kOutput, calls=%fused_computation.21 | convolution fusion | flops 4301258752 | bytes 18886656 | tf_op jit(solution)/shard_map/dot_general | solution.py:29
  563.7 15.1 %convolution_convert_fusion.1 = bf16[2048,1024]{1,0:T(8,128)(2,1)} fusion(f32[2048,1024]{1,0:T(8,128)} %fusion.14, bf16[1,1024,1024]{2,1,0:T(8,128)(2,1)} %param.16, bf16[1,2,1024,1024]{3,2,1,0:T(8,128)(2,1)} %param.15, f32[2048,1024]{1,0:T(8,128)} %copy-done.4, f32[1024]{0:T(1024)S(1)} %bitcast.74, f32[2048]{0:T(1024)S(1)} %add_rsqrt_fusion), kind=kOutput, calls=%fused_computation.15 | convolution fusion | flops 8610906112 | bytes 25178112 | tf_op jit(solution)/shard_map/dot_general | solution.py:96
  578.9 0.0 copy-start.1
  578.9 0.0 reduce-scatter.2.cloned.1.call-update
  578.9 48.2 %reduce-scatter.2.cloned.1.call-done = bf16[2048,256]{1,0:T(8,128)(2,1)} async-done(((bf16[2048,1024]{1,0:T(8,128)(2,1)}), bf16[2048,256]{1,0:T(8,128)(2,1)}) %reduce-scatter.2.cloned.1.call-update) | async-done | bytes 1048592 | tf_op jit(solution)/shard_map/reduce_scatter | solution.py:97
  627.2 3.4 add_bitcast_fusion
  630.6 0.0 copy-done.1
  (7 shorter events, 0.1 us)
Async XLA Ops:
  6.5 43.3 %copy-start = (bf16[1,1024,1024]{2,1,0:T(8,128)(2,1)S(1)}, bf16[1,1024,1024]{2,1,0:T(8,128)(2,1)}, u32[]{:S(2)}) copy-start(bf16[1,1024,1024]{2,1,0:T(8,128)(2,1)} %param.11) | copy-start | bytes 6291460
  6.5 43.3 %all-gather.6.cloned.1.call-start = ((), (), s32[]{:S(2)}) async-start(), calls=%async_computation.1 | async-start | bytes 4456448 | tf_op jit(solution)/shard_map/all_gather | solution.py:54
  7.3 143.6 %all-reduce.2.cloned.1.call-start = ((), (), s32[]{:S(2)}) async-start(), calls=%async_computation.2 | async-start | bytes 8388608 | tf_op jit(solution)/shard_map/psum | solution.py:59
  58.2 0.7 copy-start.9
  58.2 3.5 copy-start.6
  58.2 196.5 %all-gather.8.cloned.1.call-start = ((), (), s32[]{:S(2)}) async-start(), calls=%async_computation.3 | async-start | bytes 17825792 | tf_op jit(solution)/shard_map/all_gather | solution.py:71
  58.9 3.6 collective-permute-start
  62.5 93.4 %copy-start.8 = (bf16[1,3,1024,256]{3,2,1,0:T(8,128)(2,1)S(1)}, bf16[1,3,1024,256]{3,2,1,0:T(8,128)(2,1)}, u32[]{:S(2)}) copy-start(bf16[1,3,1024,256]{3,2,1,0:T(8,128)(2,1)} %param.13) | copy-start | bytes 4718596
  150.9 5.1 copy-start.2
  150.9 5.9 copy-start.3
  162.7 185.9 %all-gather.10.cloned.1.call-start = ((), (), s32[]{:S(2)}) async-start(), calls=%async_computation.4 | async-start | bytes 17825792 | tf_op jit(solution)/shard_map/all_gather | solution.py:72
  164.1 371.8 %all-gather.12.cloned.1.call-start = ((), (), s32[]{:S(2)}) async-start(), calls=%async_computation.6 | async-start | bytes 20971520 | tf_op jit(solution)/shard_map/all_gather | solution.py:11
  370.3 7.9 %copy-start.5 = (bf16[1,256,1024]{2,1,0:T(8,128)(2,1)S(1)}, bf16[1,256,1024]{2,1,0:T(8,128)(2,1)}, u32[]{:S(2)}) copy-start(bf16[1,256,1024]{2,1,0:T(8,128)(2,1)} %param.14) | copy-start | bytes 1572868
  381.4 245.8 %reduce-scatter.2.cloned.1.call-start = ((), (), s32[]{:S(2)}) async-start(), calls=%async_computation.5 | async-start | bytes 5242880 | tf_op jit(solution)/shard_map/reduce_scatter | solution.py:97
  547.9 9.1 %copy-start.7 = (bf16[1,2,1024,1024]{3,2,1,0:T(8,128)(2,1)S(1)}, bf16[1,2,1024,1024]{3,2,1,0:T(8,128)(2,1)}, u32[]{:S(2)}) copy-start(bf16[1,2,1024,1024]{3,2,1,0:T(8,128)(2,1)} %param.15) | copy-start | bytes 12582916
  553.8 3.2 copy-start.4
  578.9 51.7 %copy-start.1 = (bf16[1,1024,1024]{2,1,0:T(8,128)(2,1)S(1)}, bf16[1,1024,1024]{2,1,0:T(8,128)(2,1)}, u32[]{:S(2)}) copy-start(bf16[1,1024,1024]{2,1,0:T(8,128)(2,1)} %param.11) | copy-start | bytes 6291460
Sparse Core Ops, SparseCore 0:
  9.0 40.7 all-gather.5
  58.3 92.5 all-reduce.1
  162.8 91.8 all-gather.7
  256.2 92.3 all-gather.9
  381.5 154.2 all-gather.11
  579.0 48.0 reduce-scatter.1
